TPU v7x, 32 devices: a whole 2x2x4 slice. The times are simulated.
32 devices in a mesh: dp: 4 (over z), ctx: 4 (over y, x), tensor: 2 (over core).
Axes of the slice: x: 2, y: 2, z: 4, core: 2. Of those that a mesh axis runs over, the one named last changes fastest.
Arguments:
- tokens: bfloat16 [4096, 1024], P(('dp', 'ctx')), may hold values from -6 to 6
- doc_lengths: int32 [4, 8], P('dp'), may hold values from 1 to 512, 1024 in all within a row
- gain_attn: bfloat16 [1024], P('dp'), may hold values from 0.5 to 1.5
- w_qkv: bfloat16 [3, 1024, 1024], P(None, 'dp', 'tensor'), may hold values from -0.1875 to 0.1875
- w_attn_out: bfloat16 [1024, 1024], P('tensor', 'dp'), may hold values from -0.5 to 0.5
- gain_mlp: bfloat16 [1024], P('dp'), may hold values from 0.5 to 1.5
- w_in: bfloat16 [2, 1024, 2624], P(None, 'dp', 'tensor'), may hold values from -0.1875 to 0.1875
- w_mlp_out: bfloat16 [2624, 1024], P('tensor', 'dp'), may hold values from -0.125 to 0.125
- cotangent: bfloat16 [4096, 1024], P(('dp', 'ctx')), may hold values from -6 to 6
Outputs:
- out_tokens: bfloat16 [4096, 1024], P(('dp', 'ctx'))
- grad_tokens: float32 [4096, 1024], P(('dp', 'ctx'))
- grad_gain_attn: float32 [1024], P('dp')
- grad_w_qkv: float32 [3, 1024, 1024], P(None, 'dp', 'tensor')
- grad_w_attn_out: float32 [1024, 1024], P('tensor', 'dp')
- grad_gain_mlp: float32 [1024], P('dp')
- grad_w_in: float32 [2, 1024, 2624], P(None, 'dp', 'tensor')
- grad_w_mlp_out: float32 [2624, 1024], P('tensor', 'dp')
Inputs may be any that keep to these rules, and one draw needn't show every extreme that they name: `doc_lengths`: each row sums to 1024, and the longest document of each row has exactly half of 1024 tokens.
All inputs are finite; a program needn't handle non-finite values.
Results may differ from a plain program's by a relative error of at most 0.013.
Values may be sent and summed in bfloat16 or wider, within the bound.
A program may use at most 128 MiB of HBM per device.

v0:
```python
import math
import jax
import jax.numpy as jnp
from jax import lax
from jax.sharding import PartitionSpec as P

HD = 64
NORM_EPS = 1e-05
ROPE_BASE = 160000.0
MASK_FILL = -1e30
INV_ROOT_TWO = 1.0 / math.sqrt(2.0)
INV_ROOT_TWO_PI = 1.0 / math.sqrt(2.0 * math.pi)


def norm_forward(x_float, gain_vec):
    row_mean = jnp.mean(x_float, axis=-1, keepdims=True)
    centered = x_float - row_mean
    inv_std = lax.rsqrt(jnp.mean(centered * centered, axis=-1, keepdims=True) + NORM_EPS)
    x_hat = centered * inv_std
    normed = (x_hat * gain_vec.astype(jnp.float32)).astype(jnp.bfloat16)
    return (x_hat, inv_std, normed)


def norm_backward(grad_out, x_hat, inv_std, gain_vec):
    grad_hat = grad_out * gain_vec.astype(jnp.float32)
    grad_gain = jnp.sum(grad_out * x_hat, axis=0)
    inner_term = (
        grad_hat
        - jnp.mean(grad_hat, axis=-1, keepdims=True)
        - x_hat * jnp.mean(grad_hat * x_hat, axis=-1, keepdims=True)
    )
    return (inv_std * inner_term, grad_gain)


def rope_tables(doc_len, span_len, head_width):
    doc_end = jnp.cumsum(doc_len)
    doc_start = doc_end - doc_len
    places = jnp.arange(span_len, dtype=jnp.int32)
    inside = places[:, None] >= doc_start[None, :]
    begins = jnp.max(jnp.where(inside, doc_start[None, :], 0), axis=1)
    segment = jnp.sum((places[:, None] >= doc_end[None, :]).astype(jnp.int32), axis=1)
    offset = (places - begins).astype(jnp.float32)
    half_width = head_width // 2
    frequency = ROPE_BASE ** (-(jnp.arange(half_width, dtype=jnp.float32) * (2.0 / head_width)))
    angles = offset[:, None] * frequency[None, :]
    angles = jnp.concatenate([angles, angles], axis=1)
    return (jnp.cos(angles), jnp.sin(angles), segment)


def rotate(values_in, cosines, sines):
    half_width = values_in.shape[-1] // 2
    turned = jnp.concatenate([-values_in[..., half_width:], values_in[..., :half_width]], axis=-1)
    return values_in * cosines[:, None, :] + turned * sines[:, None, :]


def rotate_back(grads_in, cosines, sines):
    half_width = grads_in.shape[-1] // 2
    scaled = grads_in * sines[:, None, :]
    turned = jnp.concatenate([scaled[..., half_width:], -scaled[..., :half_width]], axis=-1)
    return grads_in * cosines[:, None, :] + turned


def masked_scores(query_blk, keys_all, same_doc):
    score_scale = query_blk.shape[-1] ** (-0.5)
    scores = (
        jnp.einsum("bhe,che->hbc", query_blk, keys_all, preferred_element_type=jnp.float32)
        * score_scale
    )
    return jnp.where(same_doc[None, :, :], scores, MASK_FILL)


def attend_rows(query_blk, keys_all, vals_all, same_doc):
    scores = masked_scores(query_blk, keys_all, same_doc)
    row_max = jnp.max(scores, axis=-1, keepdims=True)
    expo_vals = jnp.exp(scores - row_max)
    row_total = jnp.sum(expo_vals, axis=-1, keepdims=True)
    prob_b = (expo_vals / row_total).astype(jnp.bfloat16)
    out_rows = jnp.einsum("hbc,che->bhe", prob_b, vals_all, preferred_element_type=jnp.float32)
    log_total = (row_max + jnp.log(row_total))[:, :, 0]
    return (out_rows.astype(jnp.bfloat16), log_total)


def attend_rows_back(query_blk, out_blk, grad_blk, log_blk, keys_all, vals_all, same_doc):
    score_scale = query_blk.shape[-1] ** (-0.5)
    scores = masked_scores(query_blk, keys_all, same_doc)
    probs = jnp.exp(scores - log_blk[:, :, None])
    prob_b = probs.astype(jnp.bfloat16)
    grad_vals = jnp.einsum("hbc,bhe->che", prob_b, grad_blk, preferred_element_type=jnp.float32)
    grad_prob = jnp.einsum("bhe,che->hbc", grad_blk, vals_all, preferred_element_type=jnp.float32)
    delta_row = jnp.sum(grad_blk.astype(jnp.float32) * out_blk.astype(jnp.float32), axis=-1).T
    grad_score = (probs * (grad_prob - delta_row[:, :, None]) * score_scale).astype(jnp.bfloat16)
    grad_query = jnp.einsum(
        "hbc,che->bhe", grad_score, keys_all, preferred_element_type=jnp.float32
    )
    grad_keys = jnp.einsum(
        "hbc,bhe->che", grad_score, query_blk, preferred_element_type=jnp.float32
    )
    return (grad_query, grad_keys, grad_vals)


BOTH = ("dp", "ctx")


def add_pair(part):
    part_b = part.astype(jnp.bfloat16)
    ways = lax.axis_size("tensor")
    total = part_b.astype(jnp.float32)
    for step in range(1, ways):
        pairs = [(src, (src + step) % ways) for src in range(ways)]
        total = total + lax.ppermute(part_b, "tensor", pairs).astype(jnp.float32)
    return total


def own_rows(block, axis):
    ways = lax.axis_size("ctx")
    rows = block.shape[axis] // ways
    return lax.dynamic_slice_in_dim(block, lax.axis_index("ctx") * rows, rows, axis)


def local(tokens, doc_lengths, gain_attn, w_qkv, w_attn_out, gain_mlp, w_in, w_mlp_out, cotangent):
    f32 = jnp.float32
    bf16 = jnp.bfloat16
    gains = lax.all_gather(jnp.stack([gain_attn, gain_mlp]), "dp", axis=1, tiled=True)
    gain_one, gain_two = (gains[0], gains[1])
    w_query_all = lax.all_gather(own_rows(w_qkv, 1), BOTH, axis=1, tiled=True)
    w_out_all = lax.all_gather(own_rows(w_attn_out.T, 0), BOTH, axis=0, tiled=True)
    w_in_all = lax.all_gather(own_rows(w_in, 1), BOTH, axis=1, tiled=True)
    w_down_all = lax.all_gather(own_rows(w_mlp_out.T, 0), BOTH, axis=0, tiled=True)
    ctx_ways = lax.axis_size("ctx")
    tok_rows = tokens.shape[0]
    span_len = tok_rows * ctx_ways
    local_width = w_query_all.shape[2]
    per_group = local_width // ctx_ways
    heads_here = per_group // HD
    cosines, sines, segment = rope_tables(doc_lengths[0], span_len, HD)
    same_doc = segment[:, None] == segment[None, :]
    x_float = tokens.astype(f32)
    hat_one, inv_one, normed_one = norm_forward(x_float, gain_one)
    projected = jnp.einsum(
        "td,kde->kte", normed_one, w_query_all, preferred_element_type=f32
    ).astype(bf16)
    projected = projected.reshape(3, tok_rows, ctx_ways, per_group)
    spread = lax.all_to_all(projected, "ctx", split_axis=2, concat_axis=1, tiled=True)
    spread = spread.reshape(3, span_len, heads_here, HD)
    query_rot = rotate(spread[0].astype(f32), cosines, sines).astype(bf16)
    keys_all = rotate(spread[1].astype(f32), cosines, sines).astype(bf16)
    vals_all = spread[2]
    attn_heads, log_rows = attend_rows(query_rot, keys_all, vals_all, same_doc)
    returned = lax.all_to_all(
        attn_heads.reshape(span_len, 1, per_group), "ctx", split_axis=0, concat_axis=1, tiled=True
    )
    attn_flat = returned.reshape(tok_rows, local_width)
    attn_total = add_pair(jnp.einsum("te,de->td", attn_flat, w_out_all, preferred_element_type=f32))
    mixed_one = x_float + attn_total
    hat_two, inv_two, normed_two = norm_forward(mixed_one, gain_two)
    pair_in = jnp.einsum("td,kde->kte", normed_two, w_in_all, preferred_element_type=f32)
    act_in = pair_in[0]
    gate_in = pair_in[1]
    cdf_val = 0.5 * (1.0 + jax.scipy.special.erf(act_in * INV_ROOT_TWO))
    gelu_val = act_in * cdf_val
    hidden = (gelu_val * gate_in).astype(bf16)
    mlp_total = add_pair(jnp.einsum("tf,df->td", hidden, w_down_all, preferred_element_type=f32))
    result = (mixed_one + mlp_total).astype(bf16)
    cot_float = cotangent.astype(f32)
    grad_mlp_out = jnp.einsum("td,tf->df", cotangent, hidden, preferred_element_type=f32)
    share_down = lax.psum_scatter(grad_mlp_out.astype(bf16), BOTH, scatter_dimension=0, tiled=True)
    grad_hidden = jnp.einsum("td,df->tf", cotangent, w_down_all, preferred_element_type=f32)
    gelu_slope = cdf_val + act_in * jnp.exp(-0.5 * act_in * act_in) * INV_ROOT_TWO_PI
    grad_pair = jnp.stack(
        [(grad_hidden * gate_in * gelu_slope).astype(bf16), (grad_hidden * gelu_val).astype(bf16)]
    )
    grad_in = [
        jnp.einsum("td,te->de", normed_two, grad_pair[k], preferred_element_type=f32)
        for k in range(2)
    ]
    share_in = [
        lax.psum_scatter(grad_in[k].astype(bf16), BOTH, scatter_dimension=0, tiled=True)
        for k in range(2)
    ]
    grad_normed_two = add_pair(
        jnp.einsum("kte,kde->td", grad_pair, w_in_all, preferred_element_type=f32)
    )
    back_two, grad_gain_mlp = norm_backward(grad_normed_two, hat_two, inv_two, gain_two)
    grad_mixed = cot_float + back_two
    grad_mixed_b = grad_mixed.astype(bf16)
    grad_attn_out = jnp.einsum("td,te->de", grad_mixed_b, attn_flat, preferred_element_type=f32)
    share_out = lax.psum_scatter(grad_attn_out.astype(bf16), BOTH, scatter_dimension=0, tiled=True)
    grad_local = jnp.einsum(
        "td,de->te", grad_mixed_b, w_out_all, preferred_element_type=f32
    ).astype(bf16)
    grad_spread = lax.all_to_all(
        grad_local.reshape(tok_rows, ctx_ways, per_group),
        "ctx",
        split_axis=1,
        concat_axis=0,
        tiled=True,
    )
    grad_heads = grad_spread.reshape(span_len, heads_here, HD)
    grad_query, grad_keys, grad_vals = attend_rows_back(
        query_rot, attn_heads, grad_heads, log_rows, keys_all, vals_all, same_doc
    )
    grad_query = rotate_back(grad_query, cosines, sines).astype(bf16)
    grad_keys = rotate_back(grad_keys, cosines, sines).astype(bf16)
    grad_stack = jnp.stack([grad_query, grad_keys, grad_vals.astype(bf16)]).reshape(
        3, span_len, 1, per_group
    )
    grad_back = lax.all_to_all(grad_stack, "ctx", split_axis=1, concat_axis=2, tiled=True)
    grad_proj = grad_back.reshape(3, tok_rows, local_width)
    grad_qkv = [
        jnp.einsum("td,te->de", normed_one, grad_proj[k], preferred_element_type=f32)
        for k in range(3)
    ]
    share_qkv = lax.psum_scatter(
        jnp.concatenate(grad_qkv, axis=1).astype(bf16), BOTH, scatter_dimension=0, tiled=True
    )
    share_qkv = share_qkv.reshape(-1, 3, local_width).transpose(1, 0, 2)
    grad_normed_one = add_pair(
        jnp.einsum("kte,kde->td", grad_proj, w_query_all, preferred_element_type=f32)
    )
    back_one, grad_gain_attn = norm_backward(grad_normed_one, hat_one, inv_one, gain_one)
    grad_tok = grad_mixed + back_one
    gain_sums = lax.psum(jnp.stack([grad_gain_attn, grad_gain_mlp]), BOTH)
    gain_rows = gain_attn.shape[0]
    gain_own = lax.dynamic_slice_in_dim(gain_sums, lax.axis_index("dp") * gain_rows, gain_rows, 1)
    own_down = lax.all_gather(share_down, "ctx", axis=0, tiled=True).astype(f32).T
    own_in = lax.all_gather(jnp.stack(share_in), "ctx", axis=1, tiled=True).astype(f32)
    own_out = lax.all_gather(share_out, "ctx", axis=0, tiled=True).astype(f32).T
    own_qkv = lax.all_gather(share_qkv, "ctx", axis=1, tiled=True).astype(f32)
    return (result, grad_tok, gain_own[0], own_qkv, own_out, gain_own[1], own_in, own_down)


def solution(mesh):
    in_specs = (
        P(("dp", "ctx"), None),
        P("dp", None),
        P("dp"),
        P(None, "dp", "tensor"),
        P("tensor", "dp"),
        P("dp"),
        P(None, "dp", "tensor"),
        P("tensor", "dp"),
        P(("dp", "ctx"), None),
    )
    out_specs = (
        P(("dp", "ctx"), None),
        P(("dp", "ctx"), None),
        P("dp"),
        P(None, "dp", "tensor"),
        P("tensor", "dp"),
        P("dp"),
        P(None, "dp", "tensor"),
        P("tensor", "dp"),
    )
    return jax.shard_map(local, mesh=mesh, in_specs=in_specs, out_specs=out_specs, check_vma=False)
```

profile of v0, /device:TPU:0, one launch (start us, length us, event | category | flops | bytes accessed | tf_op | source)
XLA Modules:
  0.0 824.5 jit_solution(13252264614928242169)
XLA Ops:
  14.1 12.7 %all_gather.28 = bf16[2,1024]{1,0:T(2,128)(2,1)S(1)} all-gather(bf16[2,256]{1,0:T(2,128)(2,1)S(1)} %pad_maximum_fusion.5), channel_id=1, replica_groups=mesh['dp'=4,'ctx'=4,'tensor'=2] {'dp'}, dimensions={1}, use_global_device_ids=true | all-gather | bytes 5120 | tf_op jit(solution)/shard_map/all_gather | solution.py:123
  26.9 55.1 %all-gather.6.cloned.1.call-done = bf16[3,1024,512]{2,1,0:T(8,128)(2,1)} async-done(((bf16[3,64,512]{2,1,0:T(8,128)(2,1)}), bf16[3,1024,512]{2,1,0:T(8,128)(2,1)}) %all-gather.6.cloned.1.call-update) | async-done | bytes 3145744 | tf_op jit(solution)/shard_map/all_gather | solution.py:125
  91.2 7.8 all-to-all-done
  115.1 8.7 %all_to_all.60 = bf16[4,2,16384]{2,1,0:T(2,128)(2,1)S(1)} all-to-all(bf16[4,2,16384]{2,1,0:T(2,128)(2,1)S(1)} %reshape.237), channel_id=1, replica_groups=mesh['dp'=4,'ctx'=4,'tensor'=2] {'ctx'}, dimensions={0} | all-to-all | bytes 524288 | tf_op jit(solution)/shard_map/all_to_all | solution.py:149
  124.3 17.6 %all-gather.8.cloned.1.call-done = bf16[1024,512]{1,0:T(8,128)(2,1)} async-done(((bf16[64,512]{1,0:T(8,128)(2,1)}), bf16[1024,512]{1,0:T(8,128)(2,1)}) %all-gather.8.cloned.1.call-update) | async-done | bytes 1048592 | tf_op jit(solution)/shard_map/all_gather | solution.py:126
  146.1 86.8 %all-gather.10.cloned.1.call-done = bf16[2,1024,1312]{2,1,0:T(8,128)(2,1)} async-done(((bf16[2,64,1312]{2,1,0:T(8,128)(2,1)}), bf16[2,1024,1312]{2,1,0:T(8,128)(2,1)}) %all-gather.10.cloned.1.call-update) | async-done | bytes 5373968 | tf_op jit(solution)/shard_map/all_gather | solution.py:127
  232.8 6.0 convolution_bitcast_fusion
  238.9 61.3 %all-gather.12.cloned.1.call-done = bf16[1024,1312]{1,0:T(8,128)(2,1)} async-done(((bf16[64,1312]{1,0:T(8,128)(2,1)}), bf16[1024,1312]{1,0:T(8,128)(2,1)}) %all-gather.12.cloned.1.call-update) | async-done | bytes 2686992 | tf_op jit(solution)/shard_map/all_gather | solution.py:128
  300.2 4.9 fusion.13
  312.6 5.0 fusion.17
  337.1 9.5 %all-to-all-done.2 = bf16[256,4,128]{0,2,1:T(8,128)(2,1)S(1)} async-done(((bf16[256,4,128]{0,2,1:T(8,128)(2,1)}), bf16[256,4,128]{0,2,1:T(8,128)(2,1)S(1)}, u32[]{:S(2)}, u32[]{:S(2)}) %all-to-all-start.2) | async-done | bytes 262176 | tf_op jit(solution)/shard_map/all_to_all | solution.py:191
  347.0 6.6 fusion.28
  356.1 6.8 multiply_convert_fusion
  367.7 23.4 %reduce-scatter.12.cloned.1.call-done = bf16[64,1312]{1,0:T(8,128)(2,1)} async-done(((bf16[1024,1312]{1,0:T(8,128)(2,1)}), bf16[64,1312]{1,0:T(8,128)(2,1)}) %reduce-scatter.12.cloned.1.call-update) | async-done | bytes 167952 | tf_op jit(solution)/shard_map/reduce_scatter | solution.py:177
  391.1 84.0 %reduce-scatter.14.cloned.1.call-done = bf16[64,1312]{1,0:T(8,128)(2,1)} async-done(((bf16[1024,1312]{1,0:T(8,128)(2,1)}), bf16[64,1312]{1,0:T(8,128)(2,1)}) %reduce-scatter.14.cloned.1.call-update) | async-done | bytes 167952 | tf_op jit(solution)/shard_map/reduce_scatter | solution.py:177
  480.3 15.1 %all_to_all.61 = bf16[3,1024,1,128]{3,0,2,1:T(4,128)(2,1)S(1)} all-to-all(bf16[3,1024,1,128]{3,0,2,1:T(4,128)(2,1)S(1)} %pad_maximum_fusion.1), channel_id=1, replica_groups=mesh['dp'=4,'ctx'=4,'tensor'=2] {'ctx'}, dimensions={1} | all-to-all | bytes 1572864 | tf_op jit(solution)/shard_map/all_to_all | solution.py:207
  499.6 4.7 copy.205
  511.8 38.5 %psum.7 = f32[2,1024]{1,0:T(2,128)S(1)} all-reduce(f32[2,1024]{1,0:T(2,128)S(1)} %pad_maximum_fusion.4), channel_id=1, replica_groups=mesh['dp'=4,'ctx'=4,'tensor'=2] {'dp','ctx'}, use_global_device_ids=true, to_apply=%region_16.17 | all-reduce | flops 2048 | bytes 16384 | tf_op jit(solution)/shard_map/psum | solution.py:222
  553.9 9.5 %all_gather.33 = bf16[256,512]{1,0:T(8,128)(2,1)S(1)} all-gather(bf16[64,512]{1,0:T(8,128)(2,1)} %reduce-scatter.10.cloned.1.call-done), channel_id=1, replica_groups=mesh['dp'=4,'ctx'=4,'tensor'=2] {'ctx'}, dimensions={0}, use_global_device_ids=true | all-gather | bytes 327680 | tf_op jit(solution)/shard_map/all_gather | solution.py:227
  564.4 72.0 %reduce-scatter.18.cloned.1.call-done = bf16[64,1312]{1,0:T(8,128)(2,1)} async-done(((bf16[1024,1312]{1,0:T(8,128)(2,1)}), bf16[64,1312]{1,0:T(8,128)(2,1)}) %reduce-scatter.18.cloned.1.call-update) | async-done | bytes 167952 | tf_op jit(solution)/shard_map/reduce_scatter | solution.py:166
  636.4 11.9 %all_gather.35 = bf16[256,1312]{1,0:T(8,128)(2,1)S(1)} all-gather(bf16[64,1312]{1,0:T(8,128)(2,1)} %reduce-scatter.18.cloned.1.call-done), channel_id=1, replica_groups=mesh['dp'=4,'ctx'=4,'tensor'=2] {'ctx'}, dimensions={0}, use_global_device_ids=true | all-gather | bytes 839680 | tf_op jit(solution)/shard_map/all_gather | solution.py:225
  649.9 15.7 %all-gather.14.cloned.1.call-done = bf16[2,256,1312]{2,1,0:T(8,128)(2,1)} async-done(((bf16[2,64,1312]{2,1,0:T(8,128)(2,1)}), bf16[2,256,1312]{2,1,0:T(8,128)(2,1)}) %all-gather.14.cloned.1.call-update) | async-done | bytes 1343504 | tf_op jit(solution)/shard_map/all_gather | solution.py:226
  668.5 134.2 %reduce-scatter.16.cloned.1.call-done = bf16[64,1536]{1,0:T(8,128)(2,1)} async-done(((bf16[1024,1536]{1,0:T(8,128)(2,1)}), bf16[64,1536]{1,0:T(8,128)(2,1)}) %reduce-scatter.16.cloned.1.call-update) | async-done | bytes 196624
  804.1 12.0 %all_gather.32 = bf16[3,256,512]{2,1,0:T(8,128)(2,1)S(1)} all-gather(bf16[3,64,512]{2,1,0:T(8,128)(2,1)S(1)} %bitcast.158), channel_id=1, replica_groups=mesh['dp'=4,'ctx'=4,'tensor'=2] {'ctx'}, dimensions={1}, use_global_device_ids=true | all-gather | bytes 983040 | tf_op jit(solution)/shard_map/all_gather | solution.py:228
  (183 shorter events, 99.7 us)
Async XLA Ops:
  7.2 74.8 %all-gather.6.cloned.1.call-start = ((), (), s32[]{:S(2)}) async-start(), calls=%async_computation.9 | async-start | bytes 3342336 | tf_op jit(solution)/shard_map/all_gather | solution.py:125
  9.1 132.7 %all-gather.8.cloned.1.call-start = ((), (), s32[]{:S(2)}) async-start(), calls=%async_computation.10 | async-start | bytes 1114112 | tf_op jit(solution)/shard_map/all_gather | solution.py:126
  10.9 221.9 %all-gather.10.cloned.1.call-start = ((), (), s32[]{:S(2)}) async-start(), calls=%async_computation.11 | async-start | bytes 6127616 | tf_op jit(solution)/shard_map/all_gather | solution.py:127
  12.2 287.9 %all-gather.12.cloned.1.call-start = ((), (), s32[]{:S(2)}) async-start(), calls=%async_computation.12 | async-start | bytes 3063808 | tf_op jit(solution)/shard_map/all_gather | solution.py:128
  85.9 13.1 %all-to-all-start = ((bf16[3,256,4,128]{1,3,0,2:T(8,128)(2,1)}), bf16[3,256,4,128]{1,3,0,2:T(8,128)(2,1)S(1)}, u32[]{:S(2)}, u32[]{:S(2)}) async-start(bf16[3,256,4,128]{1,3,0,2:T(8,128)(2,1)} %copy.170), calls=%async_computation | async-start | bytes 1572864 | tf_op jit(solution)/shard_map/all_to_all | solution.py:143
  89.5 301.7 %reduce-scatter.12.cloned.1.call-start = ((), (), s32[]{:S(2)}) async-start(), calls=%async_computation.14 | async-start | bytes 3063808 | tf_op jit(solution)/shard_map/reduce_scatter | solution.py:177
  90.6 13.7 %copy-start.9 = (f32[1024,64]{0,1:T(8,128)}, f32[1024,64]{0,1:T(8,128)S(1)}, u32[]{:S(2)}) copy-start(f32[1024,64]{0,1:T(8,128)S(1)} %get-tuple-element.105) | copy-start | bytes 786436
  91.2 19.4 %copy-start.6 = (pred[1024,1024]{0,1:T(8,128)(4,1)}, pred[1024,1024]{0,1:T(8,128)(4,1)S(1)}, u32[]{:S(2)}) copy-start(pred[1024,1024]{0,1:T(8,128)(4,1)S(1)} %broadcast_compare_fusion) | copy-start | bytes 3145732
  113.5 10.3 %copy-start.15 = (bf16[2,64,1024]{2,1,0:T(8,128)(2,1)}, bf16[2,64,1024]{2,1,0:T(8,128)(2,1)S(1)}, u32[]{:S(2)}) copy-start(bf16[2,64,1024]{2,1,0:T(8,128)(2,1)S(1)} %fusion.27) | copy-start | bytes 786436
  143.6 2.0 collective-permute-start
  232.8 67.3 %copy-start.11 = (bf16[256,1024]{1,0:T(8,128)(2,1)S(1)}, bf16[256,1024]{1,0:T(8,128)(2,1)}, u32[]{:S(2)}) copy-start(bf16[256,1024]{1,0:T(8,128)(2,1)} %param.17) | copy-start | bytes 1572868
  305.0 12.7 %copy-start.8 = (bf16[256,1312]{0,1:T(8,128)(2,1)}, bf16[256,1312]{0,1:T(8,128)(2,1)S(1)}, u32[]{:S(2)}) copy-start(bf16[256,1312]{0,1:T(8,128)(2,1)S(1)} %get-tuple-element.82) | copy-start | bytes 2015236
  308.6 166.5 %reduce-scatter.14.cloned.1.call-start = ((), (), s32[]{:S(2)}) async-start(), calls=%async_computation.15 | async-start | bytes 3063808 | tf_op jit(solution)/shard_map/reduce_scatter | solution.py:177
  312.6 241.3 %reduce-scatter.10.cloned.1.call-start = ((), (), s32[]{:S(2)}) async-start(), calls=%async_computation.13 | async-start | bytes 1114112 | tf_op jit(solution)/shard_map/reduce_scatter | solution.py:187
  317.6 2.0 collective-permute-start.2
  318.8 2.1 collective-permute-start.1
  324.6 311.9 %reduce-scatter.18.cloned.1.call-start = ((), (), s32[]{:S(2)}) async-start(), calls=%async_computation.18 | async-start | bytes 3063808 | tf_op jit(solution)/shard_map/reduce_scatter | solution.py:166
  329.8 17.2 %copy-start.7 = (pred[1024,1024]{0,1:T(8,128)(4,1)S(1)}, pred[1024,1024]{0,1:T(8,128)(4,1)}, u32[]{:S(2)}) copy-start(pred[1024,1024]{0,1:T(8,128)(4,1)} %copy-done.6) | copy-start | bytes 3145732
  333.6 13.0 %all-to-all-start.2 = ((bf16[256,4,128]{0,2,1:T(8,128)(2,1)}), bf16[256,4,128]{0,2,1:T(8,128)(2,1)S(1)}, u32[]{:S(2)}, u32[]{:S(2)}) async-start(bf16[256,4,128]{0,2,1:T(8,128)(2,1)} %bitcast.26), calls=%async_computation.2 | async-start | bytes 524288 | tf_op jit(solution)/shard_map/all_to_all | solution.py:191
  337.0 328.5 %all-gather.14.cloned.1.call-start = ((), (), s32[]{:S(2)}) async-start(), calls=%async_computation.16 | async-start | bytes 1802240 | tf_op jit(solution)/shard_map/all_gather | solution.py:226
  356.0 6.8 copy-start.14
  477.0 325.7 %reduce-scatter.16.cloned.1.call-start = ((), (), s32[]{:S(2)}) async-start(), calls=%async_computation.17 | async-start | bytes 3342336
  509.3 2.0 collective-permute-start.3
  665.5 151.9 %copy-start.1 = (bf16[2,256,1312]{1,2,0:T(8,128)(2,1)S(1)}, bf16[2,256,1312]{1,2,0:T(8,128)(2,1)}, u32[]{:S(2)}) copy-start(bf16[2,256,1312]{1,2,0:T(8,128)(2,1)} %param.15) | copy-start | bytes 4030468
  (17 other events, 65.6 us)
Sparse Core Ops, SparseCore 0:
  11.4 70.5 all-gather.5
  85.3 56.4 all-gather.7
  145.2 87.6 all-gather.9
  235.4 64.6 all-gather.11
  308.8 82.3 reduce-scatter.11
  393.3 81.8 reduce-scatter.13
  478.0 75.8 reduce-scatter.9
  556.2 80.2 reduce-scatter.17
  638.9 26.6 all-gather.13
  670.4 132.3 reduce-scatter.15
where the time goes:
time: 833 us; the launch traced here: 825 us
  waiting for transfers between devices  574 us (69%)
  blocking collectives  108 us (13%)
  matrix products  59.8 us (7%)
  local copies, waits for them, and re-layouts  37.5 us (5%)
  other arithmetic  21.4 us (3%)
  between operations  15.1 us (2%)
  starting transfers between devices  8.46 us (1%)
    unnamed x11, waiting for transfers between devices  134 us
    reduce_scatter x2, waiting for transfers between devices, local(): lax.psum_scatter(grad_in[k].astype(bf16), BOTH, scatter_dimension=0, tile...  107 us
    all_gather x1, waiting for transfers between devices, local(): w_in_all = lax.all_gather(own_rows(w_in, 1), BOTH, axis=1, tiled=True)  86.8 us
    reduce_scatter x1, waiting for transfers between devices, local(): lax.psum_scatter(grad_mlp_out.astype(bf16), BOTH, scatter_dimension=0, ti...  72 us
    all_gather x1, waiting for transfers between devices, local(): lax.all_gather(own_rows(w_mlp_out.T, 0), BOTH, axis=0, tiled=True)  61.3 us
    all_gather x1, waiting for transfers between devices, local(): w_query_all = lax.all_gather(own_rows(w_qkv, 1), BOTH, axis=1, tiled=True)  55.1 us
    psum x1, blocking collectives, local(): gain_sums = lax.psum(jnp.stack([grad_gain_attn, grad_gain_mlp]), BOTH)  38.5 us
    unnamed x63, local copies, waits for them, and re-layouts  20.4 us
  transfers between devices with their start and end apart: 16, of which 16 were waited for; matrix products, arithmetic and copies ran while one was open for 13% of the time, Pallas kernels for 0%

commit v1 on v0

--- a/solution.py
+++ b/solution.py
@@ -219,7 +219,7 @@
     )
     back_one, grad_gain_attn = norm_backward(grad_normed_one, hat_one, inv_one, gain_one)
     grad_tok = grad_mixed + back_one
-    gain_sums = lax.psum(jnp.stack([grad_gain_attn, grad_gain_mlp]), BOTH)
+    gain_sums = jnp.sum(lax.all_gather(jnp.stack([grad_gain_attn, grad_gain_mlp]), BOTH), axis=0)
     gain_rows = gain_attn.shape[0]
     gain_own = lax.dynamic_slice_in_dim(gain_sums, lax.axis_index("dp") * gain_rows, gain_rows, 1)
     own_down = lax.all_gather(share_down, "ctx", axis=0, tiled=True).astype(f32).T

time: 833 us -> 834 us (level)
    psum x1 -> x0, blocking collectives: 38.5 us -> none  [local(): gain_sums = lax.psum(jnp.stack([grad_gain_attn, grad_gain_mlp]), BOTH)]
    all_gather x0 -> x1, blocking collectives: none -> 37.7 us  [local(): lax.all_gather(jnp.stack([grad_gain_attn, grad_gain_mlp]), BOTH)]
where the time goes in v1:
time: 834 us; the launch traced here: 825 us
  waiting for transfers between devices  576 us (69%)
  blocking collectives  106 us (13%)
  matrix products  59.8 us (7%)
  local copies, waits for them, and re-layouts  37.5 us (4%)
  other arithmetic  21.5 us (3%)
  between operations  15.1 us (2%)
  starting transfers between devices  8.46 us (1%)
    unnamed x11, waiting for transfers between devices  134 us
    reduce_scatter x2, waiting for transfers between devices, local(): lax.psum_scatter(grad_in[k].astype(bf16), BOTH, scatter_dimension=0, tile...  107 us
    all_gather x1, waiting for transfers between devices, local(): w_in_all = lax.all_gather(own_rows(w_in, 1), BOTH, axis=1, tiled=True)  86.8 us
    reduce_scatter x1, waiting for transfers between devices, local(): lax.psum_scatter(grad_mlp_out.astype(bf16), BOTH, scatter_dimension=0, ti...  71.9 us
    all_gather x1, waiting for transfers between devices, local(): lax.all_gather(own_rows(w_mlp_out.T, 0), BOTH, axis=0, tiled=True)  61.3 us
    all_gather x1, waiting for transfers between devices, local(): w_query_all = lax.all_gather(own_rows(w_qkv, 1), BOTH, axis=1, tiled=True)  55.1 us
    all_gather x1, blocking collectives, local(): lax.all_gather(jnp.stack([grad_gain_attn, grad_gain_mlp]), BOTH)  37.7 us
    unnamed x63, local copies, waits for them, and re-layouts  20.4 us
  transfers between devices with their start and end apart: 16, of which 16 were waited for; matrix products, arithmetic and copies ran while one was open for 13% of the time, Pallas kernels for 0%

profile of v1, /device:TPU:0, one launch (start us, length us, event | category | flops | bytes accessed | tf_op | source)
XLA Modules:
  0.0 824.8 jit_solution(11328688421913101839)
XLA Ops:
  14.1 12.7 %all_gather.34 = bf16[2,1024]{1,0:T(2,128)(2,1)S(1)} all-gather(bf16[2,256]{1,0:T(2,128)(2,1)S(1)} %pad_maximum_fusion.4), channel_id=1, replica_groups=mesh['dp'=4,'ctx'=4,'tensor'=2] {'dp'}, dimensions={1}, use_global_device_ids=true | all-gather | bytes 5120 | tf_op jit(solution)/shard_map/all_gather | solution.py:123
  26.9 55.1 %all-gather.8.cloned.1.call-done = bf16[3,1024,512]{2,1,0:T(8,128)(2,1)} async-done(((bf16[3,64,512]{2,1,0:T(8,128)(2,1)}), bf16[3,1024,512]{2,1,0:T(8,128)(2,1)}) %all-gather.8.cloned.1.call-update) | async-done | bytes 3145744 | tf_op jit(solution)/shard_map/all_gather | solution.py:125
  91.2 7.8 all-to-all-done
  115.1 8.7 %all_to_all.60 = bf16[4,2,16384]{2,1,0:T(2,128)(2,1)S(1)} all-to-all(bf16[4,2,16384]{2,1,0:T(2,128)(2,1)S(1)} %reshape.241), channel_id=1, replica_groups=mesh['dp'=4,'ctx'=4,'tensor'=2] {'ctx'}, dimensions={0} | all-to-all | bytes 524288 | tf_op jit(solution)/shard_map/all_to_all | solution.py:149
  124.3 17.6 %all-gather.10.cloned.1.call-done = bf16[1024,512]{1,0:T(8,128)(2,1)} async-done(((bf16[64,512]{1,0:T(8,128)(2,1)}), bf16[1024,512]{1,0:T(8,128)(2,1)}) %all-gather.10.cloned.1.call-update) | async-done | bytes 1048592 | tf_op jit(solution)/shard_map/all_gather | solution.py:126
  146.1 86.8 %all-gather.12.cloned.1.call-done = bf16[2,1024,1312]{2,1,0:T(8,128)(2,1)} async-done(((bf16[2,64,1312]{2,1,0:T(8,128)(2,1)}), bf16[2,1024,1312]{2,1,0:T(8,128)(2,1)}) %all-gather.12.cloned.1.call-update) | async-done | bytes 5373968 | tf_op jit(solution)/shard_map/all_gather | solution.py:127
  232.8 6.0 convolution_bitcast_fusion
  238.9 61.3 %all-gather.14.cloned.1.call-done = bf16[1024,1312]{1,0:T(8,128)(2,1)} async-done(((bf16[64,1312]{1,0:T(8,128)(2,1)}), bf16[1024,1312]{1,0:T(8,128)(2,1)}) %all-gather.14.cloned.1.call-update) | async-done | bytes 2686992 | tf_op jit(solution)/shard_map/all_gather | solution.py:128
  300.2 4.9 fusion.13
  312.6 5.0 fusion.17
  337.1 9.5 %all-to-all-done.2 = bf16[256,4,128]{0,2,1:T(8,128)(2,1)S(1)} async-done(((bf16[256,4,128]{0,2,1:T(8,128)(2,1)}), bf16[256,4,128]{0,2,1:T(8,128)(2,1)S(1)}, u32[]{:S(2)}, u32[]{:S(2)}) %all-to-all-start.2) | async-done | bytes 262176 | tf_op jit(solution)/shard_map/all_to_all | solution.py:191
  347.0 6.6 fusion.28
  356.1 6.8 multiply_convert_fusion
  367.7 23.4 %reduce-scatter.12.cloned.1.call-done = bf16[64,1312]{1,0:T(8,128)(2,1)} async-done(((bf16[1024,1312]{1,0:T(8,128)(2,1)}), bf16[64,1312]{1,0:T(8,128)(2,1)}) %reduce-scatter.12.cloned.1.call-update) | async-done | bytes 167952 | tf_op jit(solution)/shard_map/reduce_scatter | solution.py:177
  391.1 84.0 %reduce-scatter.14.cloned.1.call-done = bf16[64,1312]{1,0:T(8,128)(2,1)} async-done(((bf16[1024,1312]{1,0:T(8,128)(2,1)}), bf16[64,1312]{1,0:T(8,128)(2,1)}) %reduce-scatter.14.cloned.1.call-update) | async-done | bytes 167952 | tf_op jit(solution)/shard_map/reduce_scatter | solution.py:177
  480.3 15.1 %all_to_all.61 = bf16[3,1024,1,128]{3,0,2,1:T(4,128)(2,1)S(1)} all-to-all(bf16[3,1024,1,128]{3,0,2,1:T(4,128)(2,1)S(1)} %pad_maximum_fusion.1), channel_id=1, replica_groups=mesh['dp'=4,'ctx'=4,'tensor'=2] {'ctx'}, dimensions={1} | all-to-all | bytes 1572864 | tf_op jit(solution)/shard_map/all_to_all | solution.py:207
  499.6 4.7 copy.205
  511.8 37.7 %all-gather.1 = f32[16,2,1024]{2,1,0:T(2,128)S(1)} all-gather(f32[1,2,1024]{2,1,0:T(2,128)S(1)} %maximum_bitcast_fusion), channel_id=2, replica_groups=mesh['dp'=4,'ctx'=4,'tensor'=2] {'dp','ctx'}, dimensions={0}, use_global_device_ids=true | all-gather | bytes 139264 | tf_op jit(solution)/shard_map/all_gather | solution.py:222
  553.8 9.5 %all_gather.41 = bf16[256,512]{1,0:T(8,128)(2,1)S(1)} all-gather(bf16[64,512]{1,0:T(8,128)(2,1)} %reduce-scatter.10.cloned.1.call-done), channel_id=1, replica_groups=mesh['dp'=4,'ctx'=4,'tensor'=2] {'ctx'}, dimensions={0}, use_global_device_ids=true | all-gather | bytes 327680 | tf_op jit(solution)/shard_map/all_gather | solution.py:227
  564.4 71.9 %reduce-scatter.18.cloned.1.call-done = bf16[64,1312]{1,0:T(8,128)(2,1)} async-done(((bf16[1024,1312]{1,0:T(8,128)(2,1)}), bf16[64,1312]{1,0:T(8,128)(2,1)}) %reduce-scatter.18.cloned.1.call-update) | async-done | bytes 167952 | tf_op jit(solution)/shard_map/reduce_scatter | solution.py:166
  636.2 10.9 %all_gather.43 = bf16[256,1312]{1,0:T(8,128)(2,1)S(1)} all-gather(bf16[64,1312]{1,0:T(8,128)(2,1)} %reduce-scatter.18.cloned.1.call-done), channel_id=1, replica_groups=mesh['dp'=4,'ctx'=4,'tensor'=2] {'ctx'}, dimensions={0}, use_global_device_ids=true | all-gather | bytes 839680 | tf_op jit(solution)/shard_map/all_gather | solution.py:225
  648.7 17.2 %all-gather.16.cloned.1.call-done = bf16[2,256,1312]{2,1,0:T(8,128)(2,1)} async-done(((bf16[2,64,1312]{2,1,0:T(8,128)(2,1)}), bf16[2,256,1312]{2,1,0:T(8,128)(2,1)}) %all-gather.16.cloned.1.call-update) | async-done | bytes 1343504 | tf_op jit(solution)/shard_map/all_gather | solution.py:226
  668.8 134.2 %reduce-scatter.16.cloned.1.call-done = bf16[64,1536]{1,0:T(8,128)(2,1)} async-done(((bf16[1024,1536]{1,0:T(8,128)(2,1)}), bf16[64,1536]{1,0:T(8,128)(2,1)}) %reduce-scatter.16.cloned.1.call-update) | async-done | bytes 196624
  804.4 12.0 %all_gather.40 = bf16[3,256,512]{2,1,0:T(8,128)(2,1)S(1)} all-gather(bf16[3,64,512]{2,1,0:T(8,128)(2,1)S(1)} %bitcast.160), channel_id=1, replica_groups=mesh['dp'=4,'ctx'=4,'tensor'=2] {'ctx'}, dimensions={1}, use_global_device_ids=true | all-gather | bytes 983040 | tf_op jit(solution)/shard_map/all_gather | solution.py:228
  (184 shorter events, 100.5 us)
Async XLA Ops:
  7.2 74.8 %all-gather.8.cloned.1.call-start = ((), (), s32[]{:S(2)}) async-start(), calls=%async_computation.9 | async-start | bytes 3342336 | tf_op jit(solution)/shard_map/all_gather | solution.py:125
  9.1 132.7 %all-gather.10.cloned.1.call-start = ((), (), s32[]{:S(2)}) async-start(), calls=%async_computation.10 | async-start | bytes 1114112 | tf_op jit(solution)/shard_map/all_gather | solution.py:126
  10.9 221.9 %all-gather.12.cloned.1.call-start = ((), (), s32[]{:S(2)}) async-start(), calls=%async_computation.11 | async-start | bytes 6127616 | tf_op jit(solution)/shard_map/all_gather | solution.py:127
  12.2 287.9 %all-gather.14.cloned.1.call-start = ((), (), s32[]{:S(2)}) async-start(), calls=%async_computation.12 | async-start | bytes 3063808 | tf_op jit(solution)/shard_map/all_gather | solution.py:128
  85.9 13.1 %all-to-all-start = ((bf16[3,256,4,128]{1,3,0,2:T(8,128)(2,1)}), bf16[3,256,4,128]{1,3,0,2:T(8,128)(2,1)S(1)}, u32[]{:S(2)}, u32[]{:S(2)}) async-start(bf16[3,256,4,128]{1,3,0,2:T(8,128)(2,1)} %copy.170), calls=%async_computation | async-start | bytes 1572864 | tf_op jit(solution)/shard_map/all_to_all | solution.py:143
  89.5 301.7 %reduce-scatter.12.cloned.1.call-start = ((), (), s32[]{:S(2)}) async-start(), calls=%async_computation.14 | async-start | bytes 3063808 | tf_op jit(solution)/shard_map/reduce_scatter | solution.py:177
  90.6 13.7 %copy-start.9 = (f32[1024,64]{0,1:T(8,128)}, f32[1024,64]{0,1:T(8,128)S(1)}, u32[]{:S(2)}) copy-start(f32[1024,64]{0,1:T(8,128)S(1)} %get-tuple-element.105) | copy-start | bytes 786436
  91.2 19.4 %copy-start.6 = (pred[1024,1024]{0,1:T(8,128)(4,1)}, pred[1024,1024]{0,1:T(8,128)(4,1)S(1)}, u32[]{:S(2)}) copy-start(pred[1024,1024]{0,1:T(8,128)(4,1)S(1)} %broadcast_compare_fusion) | copy-start | bytes 3145732
  113.5 10.3 %copy-start.15 = (bf16[2,64,1024]{2,1,0:T(8,128)(2,1)}, bf16[2,64,1024]{2,1,0:T(8,128)(2,1)S(1)}, u32[]{:S(2)}) copy-start(bf16[2,64,1024]{2,1,0:T(8,128)(2,1)S(1)} %fusion.27) | copy-start | bytes 786436
  143.6 2.0 collective-permute-start
  232.8 67.3 %copy-start.11 = (bf16[256,1024]{1,0:T(8,128)(2,1)S(1)}, bf16[256,1024]{1,0:T(8,128)(2,1)}, u32[]{:S(2)}) copy-start(bf16[256,1024]{1,0:T(8,128)(2,1)} %param.17) | copy-start | bytes 1572868
  305.0 12.7 %copy-start.8 = (bf16[256,1312]{0,1:T(8,128)(2,1)}, bf16[256,1312]{0,1:T(8,128)(2,1)S(1)}, u32[]{:S(2)}) copy-start(bf16[256,1312]{0,1:T(8,128)(2,1)S(1)} %get-tuple-element.82) | copy-start | bytes 2015236
  308.6 166.5 %reduce-scatter.14.cloned.1.call-start = ((), (), s32[]{:S(2)}) async-start(), calls=%async_computation.15 | async-start | bytes 3063808 | tf_op jit(solution)/shard_map/reduce_scatter | solution.py:177
  312.6 241.3 %reduce-scatter.10.cloned.1.call-start = ((), (), s32[]{:S(2)}) async-start(), calls=%async_computation.13 | async-start | bytes 1114112 | tf_op jit(solution)/shard_map/reduce_scatter | solution.py:187
  317.6 2.0 collective-permute-start.2
  318.8 2.1 collective-permute-start.1
  324.6 311.7 %reduce-scatter.18.cloned.1.call-start = ((), (), s32[]{:S(2)}) async-start(), calls=%async_computation.18 | async-start | bytes 3063808 | tf_op jit(solution)/shard_map/reduce_scatter | solution.py:166
  329.8 17.2 %copy-start.7 = (pred[1024,1024]{0,1:T(8,128)(4,1)S(1)}, pred[1024,1024]{0,1:T(8,128)(4,1)}, u32[]{:S(2)}) copy-start(pred[1024,1024]{0,1:T(8,128)(4,1)} %copy-done.6) | copy-start | bytes 3145732
  333.6 13.0 %all-to-all-start.2 = ((bf16[256,4,128]{0,2,1:T(8,128)(2,1)}), bf16[256,4,128]{0,2,1:T(8,128)(2,1)S(1)}, u32[]{:S(2)}, u32[]{:S(2)}) async-start(bf16[256,4,128]{0,2,1:T(8,128)(2,1)} %bitcast.26), calls=%async_computation.2 | async-start | bytes 524288 | tf_op jit(solution)/shard_map/all_to_all | solution.py:191
  337.0 328.8 %all-gather.16.cloned.1.call-start = ((), (), s32[]{:S(2)}) async-start(), calls=%async_computation.16 | async-start | bytes 1802240 | tf_op jit(solution)/shard_map/all_gather | solution.py:226
  356.0 6.8 copy-start.14
  477.0 326.1 %reduce-scatter.16.cloned.1.call-start = ((), (), s32[]{:S(2)}) async-start(), calls=%async_computation.17 | async-start | bytes 3342336
  509.3 2.0 collective-permute-start.3
  665.9 151.9 %copy-start.1 = (bf16[2,256,1312]{1,2,0:T(8,128)(2,1)S(1)}, bf16[2,256,1312]{1,2,0:T(8,128)(2,1)}, u32[]{:S(2)}) copy-start(bf16[2,256,1312]{1,2,0:T(8,128)(2,1)} %param.15) | copy-start | bytes 4030468
  (17 other events, 65.6 us)
Sparse Core Ops, SparseCore 0:
  11.4 70.5 all-gather.7
  85.3 56.4 all-gather.9
  145.2 87.6 all-gather.11
  235.4 64.6 all-gather.13
  308.8 82.3 reduce-scatter.11
  393.3 81.8 reduce-scatter.13
  478.0 75.7 reduce-scatter.9
  556.1 80.0 reduce-scatter.17
  638.7 27.1 all-gather.15
  670.7 132.3 reduce-scatter.15
